TPU v7x, 512 devices: a whole 4x8x8 slice. The times are simulated.
512 devices in a mesh: dp: 128 (over z, y, core), shard: 4 (over x).
Axes of the slice: x: 4, y: 8, z: 8, core: 2. Of those that a mesh axis runs over, the one named last changes fastest.
Arguments:
- latent_grads: bfloat16 [128, 288, 2560], P('dp', None, 'shard'), may hold values from -132 to 132
- latent_errors: bfloat16 [128, 288, 2560], P('dp', None, 'shard'), may hold values from -3 to 3
- latent_moments: bfloat16 [288, 2560], P(None, 'shard'), may hold values from -2 to 2
- latent_coeffs: bfloat16 [2560, 32], P('shard'), may hold values from -5 to 5
- expand_grads: bfloat16 [128, 5120, 256], P('dp', 'shard'), may hold values from -132 to 132
- expand_errors: bfloat16 [128, 5120, 256], P('dp', 'shard'), may hold values from -3 to 3
- expand_moments: bfloat16 [5120, 256], P('shard'), may hold values from -2 to 2
- expand_coeffs: bfloat16 [256, 32], replicated, may hold values from -5 to 5
- gain_grads: bfloat16 [128, 256], P('dp'), may hold values from -132 to 132
- gain_moments: float32 [256], P('shard'), may hold values from -5 to 5
Outputs:
- latent_leftover: bfloat16 [128, 288, 2560], P('dp', None, 'shard')
- latent_momentum: bfloat16 [288, 2560], P(None, 'shard')
- latent_factor: bfloat16 [2560, 32], P('shard')
- expand_leftover: bfloat16 [128, 5120, 256], P('dp', 'shard')
- expand_momentum: bfloat16 [5120, 256], P('shard')
- expand_factor: bfloat16 [256, 32], replicated
- gain_momentum: float32 [256], P('shard')
All inputs are finite; a program needn't handle non-finite values.
Results may differ from a plain program's by a relative error of at most 0.0044.
The roundings to bfloat16 on the way count: a program that leaves them out, or rounds other values in their place, can miss the bound.
Values may be sent and summed in bfloat16 or wider, within the bound.
No kernel may reach another device: no remote copies, remote signals or barrier semaphores. Data moves between devices by JAX's collectives and lax.ppermute only.
A program may use at most 64 MiB of HBM per device.

v0:
```python
import jax
import jax.numpy as jnp
from jax import lax
from jax.sharding import PartitionSpec as P

NS_ITERS = 6
BETA = 0.9
EPSILON = 1e-06
HIGHEST = lax.Precision.HIGHEST


def inverse_root(gram_matrix):
    trace_sum = jnp.trace(gram_matrix) + EPSILON
    identity = jnp.eye(gram_matrix.shape[0], dtype=jnp.float32)
    root_left = gram_matrix / trace_sum
    root_right = identity
    for repeat_index in range(NS_ITERS):
        middle = 1.5 * identity - 0.5 * jnp.dot(root_right, root_left, precision=HIGHEST)
        root_left = jnp.dot(root_left, middle, precision=HIGHEST)
        root_right = jnp.dot(middle, root_right, precision=HIGHEST)
    return root_right / jnp.sqrt(trace_sum)


def self_gram(matrix):
    return jnp.dot(matrix.T, matrix, precision=HIGHEST)


def finish(combined, basis_rows, right_sum, moments, replicas):
    factor = (right_sum / replicas).astype(jnp.bfloat16)
    approx = jnp.einsum("nr,mr->nm", basis_rows, factor, preferred_element_type=jnp.float32)
    leftover = (combined - approx).astype(jnp.bfloat16)[None]
    momentum = (BETA * moments.astype(jnp.float32) + approx).astype(jnp.bfloat16)
    return (leftover, momentum, factor)


def local(
    latent_grads,
    latent_errors,
    latent_moments,
    latent_coeffs,
    expand_grads,
    expand_errors,
    expand_moments,
    expand_coeffs,
    gain_grads,
    gain_moments,
):
    replicas = lax.axis_size("dp")
    latent_total = latent_grads[0].astype(jnp.float32) + latent_errors[0].astype(jnp.float32)
    latent_merged = latent_total.astype(jnp.bfloat16)
    expand_total = expand_grads[0].astype(jnp.float32) + expand_errors[0].astype(jnp.float32)
    expand_merged = expand_total.astype(jnp.bfloat16)
    latent_part = jnp.dot(latent_merged, latent_coeffs, preferred_element_type=jnp.float32)
    expand_part = jnp.dot(expand_merged, expand_coeffs, preferred_element_type=jnp.float32)
    owned_width = gain_moments.shape[0]
    offset = lax.axis_index("shard") * owned_width
    gain_vector = gain_grads[0].astype(jnp.float32)
    latent_summed = lax.psum(latent_part, ("dp", "shard"))
    gain_summed = lax.psum(gain_vector, "dp")
    expand_summed = lax.psum(expand_part, "dp")
    gain_summed = lax.dynamic_slice_in_dim(gain_summed, offset, owned_width)
    gain_momentum = BETA * gain_moments + gain_summed / replicas
    latent_basis = jnp.dot(
        latent_summed, inverse_root(self_gram(latent_summed)), precision=HIGHEST
    ).astype(jnp.bfloat16)
    expand_gram = lax.psum(self_gram(expand_summed), "shard")
    expand_basis = jnp.dot(expand_summed, inverse_root(expand_gram), precision=HIGHEST).astype(
        jnp.bfloat16
    )
    latent_qpart = jnp.einsum(
        "nm,nr->mr", latent_merged, latent_basis, preferred_element_type=jnp.float32
    )
    expand_qpart = jnp.einsum(
        "nm,nr->mr", expand_merged, expand_basis, preferred_element_type=jnp.float32
    )
    latent_right = lax.psum(latent_qpart, "dp")
    expand_right = lax.psum(expand_qpart, ("dp", "shard"))
    latent_leftover, latent_momentum, latent_factor = finish(
        latent_total, latent_basis, latent_right, latent_moments, replicas
    )
    expand_leftover, expand_momentum, expand_factor = finish(
        expand_total, expand_basis, expand_right, expand_moments, replicas
    )
    return (
        latent_leftover,
        latent_momentum,
        latent_factor,
        expand_leftover,
        expand_momentum,
        expand_factor,
        gain_momentum,
    )


def solution(mesh):
    return jax.shard_map(
        local,
        mesh=mesh,
        in_specs=(
            P("dp", None, "shard"),
            P("dp", None, "shard"),
            P(None, "shard"),
            P("shard", None),
            P("dp", "shard", None),
            P("dp", "shard", None),
            P("shard", None),
            P(),
            P("dp", None),
            P("shard"),
        ),
        out_specs=(
            P("dp", None, "shard"),
            P(None, "shard"),
            P("shard", None),
            P("dp", "shard", None),
            P("shard", None),
            P(),
            P("shard"),
        ),
        check_vma=False,
    )
```

profile of v0, /device:TPU:1, one launch (start us, length us, event | category | flops | bytes accessed | tf_op | source)
XLA Modules:
  0.0 730.6 jit_solution(8128142761487943919)
XLA Ops:
  7.2 0.0 copy-start
  7.2 0.0 all-reduce.7.cloned.1.call-start
  7.2 2.4 fusion.17
  9.6 0.0 all-reduce.7.cloned.1.call-update
  9.6 0.0 all-reduce.9.cloned.1.call-start
  9.7 0.9 fusion.19
  10.6 254.7 %psum.47 = f32[256]{0:T(256)S(1)} all-reduce(f32[256]{0:T(256)S(1)} %bitcast.99), channel_id=1, replica_groups=mesh['dp'=128,'shard'=4] {'dp'}, use_global_device_ids=true, to_apply=%region_7.8 | all-reduce | flops 256 | bytes 2048 | tf_op jit(solution)/shard_map/psum | solution.py:59
  265.3 0.0 copy-start.2
  265.3 1.3 fusion.32
  266.6 0.0 copy-start.1
  266.7 13.3 %psum.45 = f32[32,32]{1,0:T(8,128)S(1)} all-reduce(f32[32,32]{1,0:T(8,128)S(1)} %fusion.32), channel_id=1, replica_groups=mesh['dp'=128,'shard'=4] {'shard'}, use_global_device_ids=true, to_apply=%region_4.5 | all-reduce | flops 1024 | bytes 8192 | tf_op jit(solution)/shard_map/psum | solution.py:66
  279.9 0.6 select_reduce_fusion
  281.2 0.1 fusion.6
  281.3 0.1 fusion.23
  281.5 0.1 fusion.20
  281.6 0.2 fusion.5
  281.8 0.1 fusion.34
  281.9 0.1 fusion.33
  282.1 0.2 fusion.4
  282.2 0.1 fusion.36
  282.4 0.1 fusion.35
  282.5 0.2 fusion.3
  282.7 0.1 fusion.38
  282.8 0.1 fusion.37
  283.0 0.2 fusion.2
  283.1 0.1 fusion.40
  283.3 0.1 fusion.39
  283.5 0.1 fusion.1
  283.7 0.1 convolution_divide_fusion
  283.8 0.3 convolution_convert_fusion
  284.2 0.0 copy-start.13
  284.2 0.9 fusion.16
  285.1 0.0 all-reduce.9.cloned.1.call-update
  285.1 0.0 all-reduce.5.cloned.1.call-start
  285.2 0.6 multiply_add_fusion
  285.8 256.9 %all-reduce.9.cloned.1.call-done = (f32[288,32]{0,1:T(8,128)}, f32[256,32]{0,1:T(8,128)}) async-done(((f32[288,32]{0,1:T(8,128)}, f32[256,32]{0,1:T(8,128)}), (f32[288,32]{0,1:T(8,128)}, f32[256,32]{0,1:T(8,128)})) %all-reduce.9.cloned.1.call-update) | async-done | bytes 69648 | tf_op jit(solution)/shard_map/psum | solution.py:58
  542.7 1.7 select_reduce_fusion.1
  545.0 0.1 fusion.12
  545.2 0.1 fusion.22
  545.3 0.1 fusion.21
  545.4 0.2 fusion.11
  545.6 0.1 fusion.25
  545.7 0.1 fusion.24
  545.9 0.2 fusion.10
  546.1 0.1 fusion.27
  546.2 0.1 fusion.26
  546.4 0.2 fusion.9
  546.5 0.1 fusion.29
  546.7 0.1 fusion.28
  546.8 0.0 copy-start.6
  546.8 0.1 fusion.8
  547.0 0.1 fusion.31
  547.1 0.1 fusion.30
  547.4 0.0 copy-start.10
  547.4 0.1 fusion.7
  547.5 0.1 convolution_divide_fusion.1
  547.7 0.2 convolution_convert_fusion.1
  547.9 0.9 fusion.18
  548.8 0.0 all-reduce.5.cloned.1.call-update
  548.8 1.6 add_convert_fusion
  550.4 171.6 %all-reduce.5.cloned.1.call-done = f32[640,32]{0,1:T(8,128)} async-done(((f32[640,32]{0,1:T(8,128)}), f32[640,32]{0,1:T(8,128)}) %all-reduce.5.cloned.1.call-update) | async-done | bytes 81936 | tf_op jit(solution)/shard_map/psum | solution.py:76
  722.0 0.9 multiply_convert_fusion
  722.9 0.0 copy-start.9
  722.9 1.2 add_convert_fusion.1
  (24 shorter events, 0.1 us)
Async XLA Ops:
  7.2 2.5 copy-start
  7.2 2.5 copy-start.4
  7.2 2.5 copy-start.3
  7.2 258.1 %all-reduce.7.cloned.1.call-start = ((), (), s32[]{:S(2)}) async-start(), calls=%async_computation.1 | async-start | bytes 327680 | tf_op jit(solution)/shard_map/psum | solution.py:60
  9.6 1.0 copy-start.12
  9.6 533.0 %all-reduce.9.cloned.1.call-start = ((), (), s32[]{:S(2)}) async-start(), calls=%async_computation.2 | async-start | bytes 163840 | tf_op jit(solution)/shard_map/psum | solution.py:58
  265.3 18.5 %copy-start.5 = (f32[1280,32]{0,1:T(8,128)S(1)}, f32[1280,32]{0,1:T(8,128)}, u32[]{:S(2)}) copy-start(f32[1280,32]{0,1:T(8,128)} %all-reduce.7.cloned.1.call-done) | copy-start | bytes 491524
  265.3 18.9 %copy-start.2 = (bf16[1,1280,256]{2,1,0:T(8,128)(2,1)S(1)}, bf16[1,1280,256]{2,1,0:T(8,128)(2,1)}, u32[]{:S(2)}) copy-start(bf16[1,1280,256]{2,1,0:T(8,128)(2,1)} %param.14) | copy-start | bytes 1966084
  266.6 17.5 %copy-start.1 = (bf16[1,1280,256]{2,1,0:T(8,128)(2,1)S(1)}, bf16[1,1280,256]{2,1,0:T(8,128)(2,1)}, u32[]{:S(2)}) copy-start(bf16[1,1280,256]{2,1,0:T(8,128)(2,1)} %param.15) | copy-start | bytes 1966084
  284.2 1.0 copy-start.13
  285.1 436.9 %all-reduce.5.cloned.1.call-start = ((), (), s32[]{:S(2)}) async-start(), calls=%async_computation | async-start | bytes 163840 | tf_op jit(solution)/shard_map/psum | solution.py:76
  542.7 4.7 copy-start.11
  542.7 5.0 copy-start.7
  546.8 2.0 copy-start.6
  547.4 3.0 copy-start.10
  548.8 174.1 %copy-start.8 = (bf16[288,640]{1,0:T(8,128)(2,1)S(1)}, bf16[288,640]{1,0:T(8,128)(2,1)}, u32[]{:S(2)}) copy-start(bf16[288,640]{1,0:T(8,128)(2,1)} %param.12) | copy-start | bytes 1105924
  722.9 1.2 copy-start.9
Sparse Core Ops, SparseCore 0:
  11.9 191.8 all-reduce.6
  285.3 257.3 all-reduce.8
  548.9 173.0 all-reduce.4
where the time goes:
time: 731 us
  waiting for transfers between devices  429 us (59%)
  blocking collectives  268 us (37%)
  matrix products  16.3 us (2%)
  between operations  15.5 us (2%)
    psum x1, waiting for transfers between devices, local(): latent_summed = lax.psum(latent_part, ('dp', 'shard'))  257 us
    psum x1, blocking collectives, local(): gain_summed = lax.psum(gain_vector, 'dp')  255 us
    psum x1, waiting for transfers between devices, local(): latent_right = lax.psum(latent_qpart, 'dp')  172 us
  transfers between devices with their start and end apart: 3, of which 2 were waited for; matrix products, arithmetic and copies ran while one was open for 0% of the time, Pallas kernels for 0%

commit v1 on v0

--- a/solution.py
+++ b/solution.py
@@ -56,7 +56,7 @@
     offset = lax.axis_index("shard") * owned_width
     gain_vector = gain_grads[0].astype(jnp.float32)
     latent_summed = lax.psum(latent_part, ("dp", "shard"))
-    gain_summed = lax.psum(gain_vector, "dp")
+    gain_summed = jnp.sum(lax.all_gather(gain_vector, "dp"), axis=0)
     expand_summed = lax.psum(expand_part, "dp")
     gain_summed = lax.dynamic_slice_in_dim(gain_summed, offset, owned_width)
     gain_momentum = BETA * gain_moments + gain_summed / replicas

time: 731 us -> 669 us (0.915)
  blocking collectives: 268 us -> 71.7 us
  waiting for transfers between devices: 429 us -> 562 us
    psum x1 -> x0, blocking collectives: 255 us -> none  [local(): gain_summed = lax.psum(gain_vector, 'dp')]
    psum x1, waiting for transfers between devices: 0.01 us -> 134 us  [local(): expand_summed = lax.psum(expand_part, 'dp')]
    all_gather x0 -> x1, blocking collectives: none -> 58.5 us  [local(): gain_summed = jnp.sum(lax.all_gather(gain_vector, 'dp'), axis=0)]
  transfers between devices with their start and end apart: 3 -> 3, of which waited for: 2 -> 3; matrix products, arithmetic and copies ran while one was open for 0% -> 0% of each run, Pallas kernels for 0% -> 0%
where the time goes in v1:
time: 669 us; the launch traced here: 668 us
  waiting for transfers between devices  562 us (84%)
  blocking collectives  71.7 us (11%)
  matrix products  16.3 us (2%)
  between operations  15.5 us (2%)
    psum x1, waiting for transfers between devices, local(): latent_summed = lax.psum(latent_part, ('dp', 'shard'))  256 us
    psum x1, waiting for transfers between devices, local(): latent_right = lax.psum(latent_qpart, 'dp')  172 us
    psum x1, waiting for transfers between devices, local(): expand_summed = lax.psum(expand_part, 'dp')  134 us
    all_gather x1, blocking collectives, local(): gain_summed = jnp.sum(lax.all_gather(gain_vector, 'dp'), axis=0)  58.5 us
  transfers between devices with their start and end apart: 3, of which 3 were waited for; matrix products, arithmetic and copies ran while one was open for 0% of the time, Pallas kernels for 0%

profile of v1, /device:TPU:1, one launch (start us, length us, event | category | flops | bytes accessed | tf_op | source)
XLA Modules:
  0.0 668.2 jit_solution(12355343234092950783)
XLA Ops:
  7.2 0.0 copy-start
  7.2 0.0 all-reduce.7.cloned.1.call-start
  7.2 2.4 fusion.17
  9.6 0.0 all-reduce.7.cloned.1.call-update
  9.6 0.0 all-reduce.9.cloned.1.call-start
  9.7 0.9 fusion.19
  10.6 58.5 %all-gather = f32[128,1,256]{2,1,0:T(1,128)S(1)} all-gather(f32[1,1,256]{2,1,0:T(1,128)S(1)} %bitcast_convert_fusion.6), channel_id=1, replica_groups=mesh['dp'=128,'shard'=4] {'dp'}, dimensions={0}, use_global_device_ids=true | all-gather | bytes 132096 | tf_op jit(solution)/shard_map/all_gather | solution.py:59
  69.1 0.2 reduce_sum.27
  69.2 134.5 %all-reduce.7.cloned.1.call-done = f32[1280,32]{0,1:T(8,128)} async-done(((f32[1280,32]{0,1:T(8,128)}), f32[1280,32]{0,1:T(8,128)}) %all-reduce.7.cloned.1.call-update) | async-done | bytes 163856 | tf_op jit(solution)/shard_map/psum | solution.py:60
  203.7 1.3 fusion.32
  205.0 0.0 copy-start.1
  205.1 13.2 %psum.38 = f32[32,32]{1,0:T(8,128)S(1)} all-reduce(f32[32,32]{1,0:T(8,128)S(1)} %fusion.32), channel_id=1, replica_groups=mesh['dp'=128,'shard'=4] {'shard'}, use_global_device_ids=true, to_apply=%region_4.5 | all-reduce | flops 1024 | bytes 8192 | tf_op jit(solution)/shard_map/psum | solution.py:66
  218.3 0.6 select_reduce_fusion
  219.6 0.1 fusion.6
  219.7 0.1 fusion.23
  219.8 0.1 fusion.20
  220.0 0.2 fusion.5
  220.1 0.1 fusion.34
  220.3 0.1 fusion.33
  220.4 0.2 fusion.4
  220.6 0.1 fusion.36
  220.7 0.1 fusion.35
  220.9 0.2 fusion.3
  221.1 0.1 fusion.38
  221.2 0.1 fusion.37
  221.3 0.2 fusion.2
  221.5 0.1 fusion.39
  221.7 0.1 fusion.40
  221.8 0.2 fusion.1
  222.0 0.1 convolution_divide_fusion
  222.1 0.3 convolution_convert_fusion
  222.5 0.9 fusion.16
  223.4 0.0 all-reduce.9.cloned.1.call-update
  223.4 0.0 all-reduce.5.cloned.1.call-start
  223.5 0.6 multiply_add_fusion
  224.1 256.2 %all-reduce.9.cloned.1.call-done = (f32[288,32]{0,1:T(8,128)}, f32[256,32]{0,1:T(8,128)}) async-done(((f32[288,32]{0,1:T(8,128)}, f32[256,32]{0,1:T(8,128)}), (f32[288,32]{0,1:T(8,128)}, f32[256,32]{0,1:T(8,128)})) %all-reduce.9.cloned.1.call-update) | async-done | bytes 69648 | tf_op jit(solution)/shard_map/psum | solution.py:58
  480.3 1.7 select_reduce_fusion.1
  482.7 0.1 fusion.12
  482.8 0.1 fusion.22
  482.9 0.1 fusion.21
  483.1 0.2 fusion.11
  483.2 0.1 fusion.25
  483.4 0.1 fusion.24
  483.5 0.2 fusion.10
  483.7 0.1 fusion.27
  483.8 0.1 fusion.26
  484.0 0.2 fusion.9
  484.2 0.1 fusion.29
  484.3 0.1 fusion.28
  484.4 0.0 copy-start.6
  484.5 0.1 fusion.8
  484.6 0.1 fusion.30
  484.8 0.1 fusion.31
  484.9 0.0 copy-done.11
  484.9 0.1 fusion.7
  485.1 0.1 convolution_divide_fusion.1
  485.3 0.2 convolution_convert_fusion.1
  485.5 0.9 fusion.18
  486.4 0.0 all-reduce.5.cloned.1.call-update
  486.4 1.6 add_convert_fusion
  488.0 171.6 %all-reduce.5.cloned.1.call-done = f32[640,32]{0,1:T(8,128)} async-done(((f32[640,32]{0,1:T(8,128)}), f32[640,32]{0,1:T(8,128)}) %all-reduce.5.cloned.1.call-update) | async-done | bytes 81936 | tf_op jit(solution)/shard_map/psum | solution.py:76
  659.6 0.9 multiply_convert_fusion
  660.5 0.0 copy-start.9
  660.5 1.2 add_convert_fusion.1
  (25 shorter events, 0.1 us)
Async XLA Ops:
  7.2 2.5 copy-start
  7.2 2.5 copy-start.3
  7.2 2.5 copy-start.4
  7.2 196.5 %all-reduce.7.cloned.1.call-start = ((), (), s32[]{:S(2)}) async-start(), calls=%async_computation.1 | async-start | bytes 327680 | tf_op jit(solution)/shard_map/psum | solution.py:60
  9.6 1.0 copy-start.12
  9.6 470.6 %all-reduce.9.cloned.1.call-start = ((), (), s32[]{:S(2)}) async-start(), calls=%async_computation.2 | async-start | bytes 163840 | tf_op jit(solution)/shard_map/psum | solution.py:58
  203.7 18.4 %copy-start.5 = (f32[1280,32]{0,1:T(8,128)S(1)}, f32[1280,32]{0,1:T(8,128)}, u32[]{:S(2)}) copy-start(f32[1280,32]{0,1:T(8,128)} %all-reduce.7.cloned.1.call-done) | copy-start | bytes 491524
  203.7 18.8 %copy-start.2 = (bf16[1,1280,256]{2,1,0:T(8,128)(2,1)S(1)}, bf16[1,1280,256]{2,1,0:T(8,128)(2,1)}, u32[]{:S(2)}) copy-start(bf16[1,1280,256]{2,1,0:T(8,128)(2,1)} %param.14) | copy-start | bytes 1966084
  205.0 17.5 %copy-start.1 = (bf16[1,1280,256]{2,1,0:T(8,128)(2,1)S(1)}, bf16[1,1280,256]{2,1,0:T(8,128)(2,1)}, u32[]{:S(2)}) copy-start(bf16[1,1280,256]{2,1,0:T(8,128)(2,1)} %param.15) | copy-start | bytes 1966084
  222.5 1.0 copy-start.13
  223.4 436.1 %all-reduce.5.cloned.1.call-start = ((), (), s32[]{:S(2)}) async-start(), calls=%async_computation | async-start | bytes 163840 | tf_op jit(solution)/shard_map/psum | solution.py:76
  480.3 4.7 copy-start.11
  480.3 5.0 copy-start.7
  484.4 1.9 copy-start.6
  484.9 3.0 copy-start.10
  486.4 174.1 %copy-start.8 = (bf16[288,640]{1,0:T(8,128)(2,1)S(1)}, bf16[288,640]{1,0:T(8,128)(2,1)}, u32[]{:S(2)}) copy-start(bf16[288,640]{1,0:T(8,128)(2,1)} %param.12) | copy-start | bytes 1105924
  660.5 1.2 copy-start.9
Sparse Core Ops, SparseCore 0:
  11.9 191.7 all-reduce.6
  223.6 256.6 all-reduce.8
  486.5 173.0 all-reduce.4
